TPU v7x, 32 devices: a whole 2x2x4 slice. The times are simulated.
32 devices in a mesh: parts: 2 (over y), seq: 4 (over z), chan: 2 (over x), rep: 2 (over core).
Axes of the slice: x: 2, y: 2, z: 4, core: 2. Of those that a mesh axis runs over, the one named last changes fastest.
Arguments:
- tokens: bfloat16 [4096, 4096], P(('parts', 'seq'), ('chan', 'rep')), parts along dimension 0, may hold values from -6 to 6
- w_query: bfloat16 [4096, 4096], P('seq', ('chan', 'rep')), may hold values from -0.09375 to 0.09375
- w_key: bfloat16 [4096, 4096], P('seq', ('chan', 'rep')), may hold values from -0.09375 to 0.09375
- w_value: bfloat16 [4096, 4096], P('seq', ('chan', 'rep')), may hold values from -0.09375 to 0.09375
- decay_rate: float32 [4096, 16], P(('chan', 'rep', 'seq')), may hold values from 4.8828125e-06 to 0.04, as said below
- residue: float32 [4096, 16], P(('chan', 'rep', 'seq')), may hold values from -1.5 to 1.5
- carried: float32 [8192, 16], P(('parts', 'chan', 'rep', 'seq')), parts along dimension 0, may hold values from -6 to 6
Outputs:
- gated_output: bfloat16 [4096, 4096], P(('parts', 'seq'), ('chan', 'rep')), parts along dimension 0
- new_state: float32 [8192, 16], P(('parts', 'chan', 'rep', 'seq')), parts along dimension 0
There are 2 independent parts, one for each index of `parts`. A program takes and returns all parts, laid end to end along the dimension named above; an argument that names none is the same for every part. Nothing has to cross between parts.
Inputs may be any that keep to these rules, and one draw needn't show every extreme that they name: `decay_rate`: each rate lies between 0.01 / 2048 and 0.04.
All inputs are finite; a program needn't handle non-finite values.
Results may differ from a plain program's by a relative error of at most 0.0066.
Values may be sent and summed in bfloat16 or wider, within the bound.
A program may use at most 128 MiB of HBM per device.

v0:
```python
import jax
import jax.numpy as jnp
from jax import lax
from jax.sharding import PartitionSpec as P

BLOCK = 128


HIGHEST_PRECISION = lax.Precision.HIGHEST


def mode_scale(decay_rates):
    return jnp.sqrt(-jnp.expm1(-2.0 * decay_rates))


def local_ends(blocks, decay_rates):
    block_width = blocks.shape[2]
    offsets = jnp.arange(block_width, dtype=jnp.float32)
    tail_powers = jnp.exp(-decay_rates[:, :, None] * (block_width - 1.0 - offsets)[None, None, :])
    sums_here = jnp.einsum("cnb,cmb->cnm", blocks, tail_powers, precision=HIGHEST_PRECISION)
    return mode_scale(decay_rates)[:, None, :] * sums_here


def combine_states(earlier, later):
    return (earlier[0] * later[0], later[0] * earlier[1] + later[1])


def block_sums(block_ends, decay_rates, block_width):
    step_decay = jnp.broadcast_to(jnp.exp(-decay_rates * block_width)[:, None, :], block_ends.shape)
    unused_decay, running = lax.associative_scan(combine_states, (step_decay, block_ends), axis=1)
    return running


def entering_states(running, decay_rates, start_state, block_width):
    count_blocks = running.shape[1]
    block_starts = jnp.arange(count_blocks, dtype=jnp.float32) * block_width
    decayed = (
        jnp.exp(-decay_rates[:, None, :] * block_starts[None, :, None]) * start_state[:, None, :]
    )
    earlier_sums = jnp.concatenate([jnp.zeros_like(running[:, :1]), running[:, :-1]], axis=1)
    final_state = (
        jnp.exp(-decay_rates * (count_blocks * block_width)) * start_state + running[:, -1]
    )
    return (decayed + earlier_sums, final_state)


def block_convolve(blocks, decay_rates, residues, entering):
    block_width = blocks.shape[2]
    offsets = jnp.arange(block_width, dtype=jnp.float32)
    powers = jnp.exp(-decay_rates[:, :, None] * offsets[None, None, :])
    kernel = jnp.sum((residues * mode_scale(decay_rates))[:, :, None] * powers, axis=1)
    out_index = jnp.arange(block_width, dtype=jnp.int32)[:, None]
    in_index = jnp.arange(block_width, dtype=jnp.int32)[None, :]
    lag = jnp.maximum(out_index - in_index, 0)
    causal = (out_index >= in_index).astype(jnp.float32)
    toeplitz = kernel[:, lag] * causal[None, :, :]
    direct = jnp.einsum("cij,cnj->cni", toeplitz, blocks, precision=HIGHEST_PRECISION)
    leading = residues[:, :, None] * jnp.exp(
        -decay_rates[:, :, None] * (offsets + 1.0)[None, None, :]
    )
    return direct + jnp.einsum("cnm,cmb->cnb", entering, leading, precision=HIGHEST_PRECISION)


def per_device(tokens, w_query, w_key, w_value, decay_rate, residue, carried):
    gathered = lax.all_gather(tokens, ("chan", "rep"), axis=1, tiled=True)
    pieces = (
        lax.all_gather(w_query, "seq", axis=0, tiled=True),
        lax.all_gather(w_key, "seq", axis=0, tiled=True),
        lax.all_gather(w_value, "seq", axis=0, tiled=True),
    )
    query_acc, key_acc, value_acc = tuple(
        (
            lax.dot_general(
                weight_piece, gathered, (((0,), (1,)), ((), ())), preferred_element_type=jnp.float32
            )
            for weight_piece in pieces
        )
    )
    query_rows = query_acc.astype(jnp.bfloat16)
    key_rows = key_acc.astype(jnp.bfloat16)
    value_rows = value_acc.astype(jnp.bfloat16)
    query_rows, key_rows, value_rows = lax.optimization_barrier((query_rows, key_rows, value_rows))
    product = (key_rows.astype(jnp.float32) * value_rows.astype(jnp.float32)).astype(jnp.bfloat16)
    owned = lax.all_to_all(product, "seq", split_axis=0, concat_axis=1, tiled=True)
    own_chan = owned.shape[0]
    blocks = owned.astype(jnp.float32).reshape(own_chan, -1, BLOCK)
    block_end = local_ends(blocks, decay_rate)
    running = block_sums(block_end, decay_rate, BLOCK)
    entering, new_state = entering_states(running, decay_rate, carried, BLOCK)
    conv_out = (
        block_convolve(blocks, decay_rate, residue, entering)
        .reshape(own_chan, -1)
        .astype(jnp.bfloat16)
    )
    conv_back = lax.all_to_all(conv_out, "seq", split_axis=1, concat_axis=0, tiled=True)
    conv_back = lax.optimization_barrier(conv_back)
    gated_rows = (query_rows.astype(jnp.float32) * conv_back.astype(jnp.float32)).astype(
        jnp.bfloat16
    )
    return (gated_rows.T, new_state)


def solution(mesh):
    in_specs = (
        P(("parts", "seq"), ("chan", "rep")),
        P("seq", ("chan", "rep")),
        P("seq", ("chan", "rep")),
        P("seq", ("chan", "rep")),
        P(("chan", "rep", "seq"), None),
        P(("chan", "rep", "seq"), None),
        P(("parts", "chan", "rep", "seq"), None),
    )
    out_specs = (P(("parts", "seq"), ("chan", "rep")), P(("parts", "chan", "rep", "seq"), None))
    return jax.shard_map(
        per_device, mesh=mesh, in_specs=in_specs, out_specs=out_specs, check_vma=False
    )
```

profile of v0, /device:TPU:0, one launch (start us, length us, event | category | flops | bytes accessed | tf_op | source)
XLA Modules:
  0.0 892.3 jit_solution(9906552894119461772)
XLA Ops:
  10.0 36.8 %all-gather.7.cloned.1.call-done = bf16[512,4096]{1,0:T(8,128)(2,1)} async-done(((bf16[512,1024]{1,0:T(8,128)(2,1)}), bf16[512,4096]{1,0:T(8,128)(2,1)}) %all-gather.7.cloned.1.call-update) | async-done | bytes 4194320 | tf_op jit(solution)/shard_map/all_gather | solution.py:65
  46.7 151.2 %all-gather.5.cloned.1.call-done = bf16[4096,1024]{1,0:T(8,128)(2,1)} async-done(((bf16[1024,1024]{1,0:T(8,128)(2,1)}), bf16[4096,1024]{1,0:T(8,128)(2,1)}) %all-gather.5.cloned.1.call-update) | async-done | bytes 8388624 | tf_op jit(solution)/shard_map/all_gather | solution.py:67
  198.0 10.1 %convolution_convert_fusion.2 = bf16[1024,512]{1,0:T(8,128)(2,1)} fusion(bf16[4096,1024]{1,0:T(8,128)(2,1)} %all-gather.5.cloned.1.call-done, bf16[512,4096]{1,0:T(8,128)(2,1)} %all-gather.7.cloned.1.call-done), kind=kOutput, calls=%fused_computation.25 | convolution fusion | flops 4295491584 | bytes 13631488 | tf_op jit(solution)/shard_map/dot_general | solution.py:73
  208.1 139.3 %all-gather.9.cloned.1.call-done = bf16[4096,1024]{1,0:T(8,128)(2,1)} async-done(((bf16[1024,1024]{1,0:T(8,128)(2,1)}), bf16[4096,1024]{1,0:T(8,128)(2,1)}) %all-gather.9.cloned.1.call-update) | async-done | bytes 8388624 | tf_op jit(solution)/shard_map/all_gather | solution.py:68
  347.4 9.1 %convolution_convert_fusion.1 = bf16[1024,512]{1,0:T(8,128)(2,1)S(1)} fusion(bf16[4096,1024]{1,0:T(8,128)(2,1)} %all-gather.9.cloned.1.call-done, bf16[512,4096]{1,0:T(8,128)(2,1)} %all-gather.7.cloned.1.call-done), kind=kOutput, calls=%fused_computation.24 | convolution fusion | flops 4295491584 | bytes 13631488 | tf_op jit(solution)/shard_map/dot_general | solution.py:73
  356.5 140.1 %all-gather.11.cloned.1.call-done = bf16[4096,1024]{1,0:T(8,128)(2,1)} async-done(((bf16[1024,1024]{1,0:T(8,128)(2,1)}), bf16[4096,1024]{1,0:T(8,128)(2,1)}) %all-gather.11.cloned.1.call-update) | async-done | bytes 8388624 | tf_op jit(solution)/shard_map/all_gather | solution.py:69
  496.6 9.3 %convolution_convert_fusion = bf16[1024,512]{1,0:T(8,128)(2,1)S(1)} fusion(bf16[4096,1024]{1,0:T(8,128)(2,1)} %all-gather.11.cloned.1.call-done, bf16[512,4096]{1,0:T(8,128)(2,1)} %all-gather.7.cloned.1.call-done), kind=kOutput, calls=%fused_computation.23 | convolution fusion | flops 4295491584 | bytes 13631488 | tf_op jit(solution)/shard_map/dot_general | solution.py:73
  506.0 1.3 multiply_convert_fusion.1
  507.3 3.5 all-to-all-start
  510.9 0.8 copy.74
  513.9 1.7 multiply_reduce_fusion
  515.7 62.0 %gather_fusion = f32[16384,256]{1,0:T(8,128)} fusion(f32[256,128]{0,1:T(8,128)S(1)} %copy.66, s32[16384]{0:T(1024)S(1)} %bitcast_clamp_fusion), kind=kCustom, calls=%fused_computation | custom fusion | bytes 33619968 | tf_op jit(solution)/shard_map/gather | solution.py:56
  577.8 18.0 %copy.67 = f32[128,128,256]{1,0,2:T(8,128)} copy(f32[128,128,256]{2,1,0:T(8,128)} %bitcast.30) | data formatting | bytes 33554432 | tf_op jit(solution)/shard_map/gather | solution.py:56
  596.4 0.8 copy.63
  597.7 2.9 fusion.16
  601.3 3.5 slice.88
  604.8 3.5 slice.108
  608.2 3.5 slice.89
  611.7 1.9 copy_add_fusion
  615.3 1.0 pad.29
  616.4 0.8 add.78
  617.4 2.0 pad.31
  621.6 77.4 %pad.32 = f32[256,16,16]{2,1,0:T(8,128)} pad(f32[256,8,16]{2,1,0:T(8,128)S(1)} %pad_maximum_fusion, f32[]{:T(128)} %constant.8.clone.1), padding=0_0_0x0_1_1x0_0_0 | pad | bytes 393220 | tf_op jit(solution)/shard_map/pad | solution.py:30
  699.0 77.5 %pad.33.clone = f32[256,16,16]{2,1,0:T(8,128)} pad(f32[256,8,16]{2,1,0:T(8,128)S(1)} %copy.81, f32[]{:T(128)} %constant.8.clone.1), padding=0_0_0x1_0_1x0_0_0 | pad | bytes 393220 | tf_op jit(solution)/shard_map/pad | solution.py:30
  776.5 2.5 slice_add_fusion
  779.1 3.0 fusion.4
  782.1 15.9 %add_convert_fusion = bf16[256,16,128]{2,1,0:T(8,128)(2,1)S(1)} fusion(f32[256,16,128]{2,1,0:T(8,128)S(1)} %fusion.4, bf16[256,16,128]{2,1,0:T(8,128)(2,1)S(1)} %reshape.72, f32[128,128,256]{1,0,2:T(8,128)} %copy.67, f32[128,128]{1,0:T(8,128)S(1)} %copy-done.8), kind=kOutput, calls=%fused_computation.7 | convolution fusion | flops 810549248 | bytes 21037056 | tf_op jit(solution)/shard_map/cij,cnj->cni/dot_general | solution.py:57
  798.4 1.2 copy.75
  799.6 5.0 all-to-all-start.1
  804.7 77.5 %pad.63 = f32[256,15,16]{2,1,0:T(8,128)} pad(f32[256,8,16]{2,1,0:T(8,128)S(1)} %copy.81, f32[]{:T(128)} %constant.8.clone.1), padding=0_0_0x0_0_1x0_0_0 | pad | bytes 376836
  882.1 1.3 slice.157
  884.5 1.3 copy.77
  (70 shorter events, 12.5 us)
Async XLA Ops:
  7.2 39.6 %all-gather.7.cloned.1.call-start = ((), (), s32[]{:S(2)}) async-start(), calls=%async_computation.3 | async-start | bytes 5242880 | tf_op jit(solution)/shard_map/all_gather | solution.py:65
  7.9 190.1 %all-gather.5.cloned.1.call-start = ((), (), s32[]{:S(2)}) async-start(), calls=%async_computation.2 | async-start | bytes 10485760 | tf_op jit(solution)/shard_map/all_gather | solution.py:67
  8.6 338.7 %all-gather.9.cloned.1.call-start = ((), (), s32[]{:S(2)}) async-start(), calls=%async_computation.4 | async-start | bytes 10485760 | tf_op jit(solution)/shard_map/all_gather | solution.py:68
  9.4 487.2 %all-gather.11.cloned.1.call-start = ((), (), s32[]{:S(2)}) async-start(), calls=%async_computation.5 | async-start | bytes 10485760 | tf_op jit(solution)/shard_map/all_gather | solution.py:69
  505.9 4.8 copy-start.11
  506.0 4.9 copy-start.10
  506.0 5.8 copy-start.12
  507.3 89.2 %all-to-all-start = ((bf16[4,256,512]{2,1,0:T(8,128)(2,1)}), bf16[4,256,512]{2,1,0:T(8,128)(2,1)S(1)}, u32[]{:S(2)}, u32[]{:S(2)}) async-start(bf16[4,256,512]{2,1,0:T(8,128)(2,1)} %bitcast), calls=%async_computation | async-start | bytes 2097152 | tf_op jit(solution)/shard_map/all_to_all | solution.py:84
  513.9 63.8 %copy-start.2 = (f32[256,16]{1,0:T(8,128)}, f32[256,16]{1,0:T(8,128)S(1)}, u32[]{:S(2)}) copy-start(f32[256,16]{1,0:T(8,128)S(1)} %get-tuple-element.23) | copy-start | bytes 49156
  611.7 2.6 copy-start.4
  616.3 0.9 copy-start.7
  619.5 1.2 copy-start
  619.7 1.7 copy-start.5
  776.5 2.6 copy-start.3
  776.5 2.6 copy-start.6
  776.5 2.6 copy-start.9
  779.0 3.0 copy-start.8
  799.6 84.6 %all-to-all-start.1 = ((bf16[256,4,512]{2,0,1:T(8,128)(2,1)}), bf16[256,4,512]{2,0,1:T(8,128)(2,1)S(1)}, u32[]{:S(2)}, u32[]{:S(2)}) async-start(bf16[256,4,512]{2,0,1:T(8,128)(2,1)} %copy.75), calls=%async_computation.1 | async-start | bytes 2097152 | tf_op jit(solution)/shard_map/all_to_all | solution.py:95
  804.7 79.5 %copy-start.1 = (bf16[1024,512]{1,0:T(8,128)(2,1)S(1)}, bf16[1024,512]{1,0:T(8,128)(2,1)}, u32[]{:S(2)}) copy-start(bf16[1024,512]{1,0:T(8,128)(2,1)} %convolution_convert_fusion.2) | copy-start | bytes 3145732
Sparse Core Ops, SparseCore 0:
  9.5 37.1 all-gather.6
  48.3 149.6 all-gather.4
  199.5 147.7 all-gather.8
  348.8 147.7 all-gather.10
where the time goes:
time: 893 us; the launch traced here: 892 us
  waiting for transfers between devices  470 us (53%)
  local copies, waits for them, and re-layouts  337 us (38%)
  matrix products  50.3 us (6%)
  between operations  14.1 us (2%)
  other arithmetic  12 us (1%)
    pad x6, local copies, waits for them, and re-layouts, block_sums(): lax.associative_scan(combine_states, (step_decay, block_ends), axis=1)  158 us
    all_gather x1, waiting for transfers between devices, per_device(): lax.all_gather(w_query, 'seq', axis=0, tiled=True)  151 us
    all_gather x1, waiting for transfers between devices, per_device(): lax.all_gather(w_value, 'seq', axis=0, tiled=True)  140 us
    all_gather x1, waiting for transfers between devices, per_device(): lax.all_gather(w_key, 'seq', axis=0, tiled=True)  139 us
    unnamed x33, local copies, waits for them, and re-layouts  82.2 us
    gather x2, local copies, waits for them, and re-layouts, block_convolve(): toeplitz = kernel[:, lag] * causal[None, :, :]  80 us
    all_gather x1, waiting for transfers between devices, per_device(): gathered = lax.all_gather(tokens, ('chan', 'rep'), axis=1, tiled=True)  36.8 us
    dot_general x3, matrix products, per_device(): lax.dot_general(weight_piece, gathered, (((0,), (1,)), ((), ())), preferr...  28.5 us
  transfers between devices with their start and end apart: 6, of which 4 were waited for; matrix products, arithmetic and copies ran while one was open for 21% of the time, Pallas kernels for 0%

commit v1 on v0

--- a/solution.py
+++ b/solution.py
@@ -1,9 +1,15 @@
+import functools
+
 import jax
 import jax.numpy as jnp
 from jax import lax
+from jax.experimental import pallas as pl
+from jax.experimental.pallas import tpu as pltpu
 from jax.sharding import PartitionSpec as P
 
 BLOCK = 128
+LANES = 128
+CHUNKS = 8
 
 
 HIGHEST_PRECISION = lax.Precision.HIGHEST
@@ -100,6 +106,117 @@
     return (gated_rows.T, new_state)
 
 
+def scan_kernel(q_ref, k_ref, v_ref, rate_ref, scale_ref, residue_ref, carried_ref, gated_ref,
+                state_ref, signal, ends, entering, conv):
+    length, width = q_ref.shape
+    modes = rate_ref.shape[0]
+    chunk = length // CHUNKS
+    rows_at = 256
+    for lane in range(0, width, LANES):
+        lanes = pl.ds(lane, LANES)
+
+        def multiply(step, _):
+            rows = pl.ds(pl.multiple_of(step * rows_at, rows_at), rows_at)
+            product = k_ref[rows, lanes].astype(jnp.float32) * v_ref[rows, lanes].astype(jnp.float32)
+            signal[rows, :] = product.astype(jnp.bfloat16).astype(jnp.float32)
+            return 0
+
+        lax.fori_loop(0, length // rows_at, multiply, 0)
+        rates = rate_ref[:, lanes]
+        residues = residue_ref[:, lanes]
+        scale = scale_ref[:, lanes]
+        decay = jnp.exp(-rates)
+        weight = residues * scale
+        chunk_decay = jnp.exp(-rates * chunk)
+
+        def rows_of(array):
+            return [jnp.broadcast_to(array[m : m + 1, :], (CHUNKS, LANES)) for m in range(modes)]
+
+        decays = rows_of(decay)
+        weights = rows_of(weight)
+
+        def sums(step, states):
+            here = signal[pl.ds(step, CHUNKS, stride=chunk), :]
+            return tuple(d * s + here for d, s in zip(decays, states))
+
+        zero = jnp.zeros((CHUNKS, LANES), jnp.float32)
+        finals = lax.fori_loop(0, chunk, sums, (zero,) * modes, unroll=4)
+        for m in range(modes):
+            ends[m] = finals[m]
+        state = carried_ref[:, lanes]
+        for c in range(CHUNKS):
+            entering[:, c, :] = residues * state
+            state = chunk_decay * state + scale * ends[:, c, :]
+        state_ref[:, lanes] = state
+
+        def outputs(step, states):
+            here = signal[pl.ds(step, CHUNKS, stride=chunk), :]
+            states = tuple(d * s + w * here for d, s, w in zip(decays, states, weights))
+            terms = list(states)
+            while len(terms) > 1:
+                terms = [a + b for a, b in zip(terms[::2], terms[1::2])] + (
+                    [terms[-1]] if len(terms) % 2 else []
+                )
+            conv[pl.ds(step, CHUNKS, stride=chunk), :] = terms[0]
+            return states
+
+        starts = tuple(entering[m] for m in range(modes))
+        lax.fori_loop(0, chunk, outputs, starts, unroll=4)
+
+        def gate(step, _):
+            rows = pl.ds(pl.multiple_of(step * rows_at, rows_at), rows_at)
+            rounded = conv[rows, :].astype(jnp.bfloat16).astype(jnp.float32)
+            gated_ref[rows, lanes] = (q_ref[rows, lanes].astype(jnp.float32) * rounded).astype(
+                jnp.bfloat16
+            )
+            return 0
+
+        lax.fori_loop(0, length // rows_at, gate, 0)
+
+
+def gated_scan(rows, rate, residue, carried):
+    length = rows.shape[0]
+    width, modes = rate.shape
+    vmem = pl.BlockSpec(memory_space=pltpu.VMEM)
+    gated, state = pl.pallas_call(
+        scan_kernel,
+        grid=(1,),
+        out_shape=(
+            jax.ShapeDtypeStruct((length, width), jnp.bfloat16),
+            jax.ShapeDtypeStruct((modes, width), jnp.float32),
+        ),
+        in_specs=[pl.BlockSpec((length, width), functools.partial(lambda j, i: (0, j), j)) for j in range(3)]
+        + [vmem] * 4,
+        out_specs=(pl.BlockSpec((length, width), lambda i: (0, 0)), vmem),
+        scratch_shapes=[
+            pltpu.VMEM((length, LANES), jnp.float32),
+            pltpu.VMEM((modes, CHUNKS, LANES), jnp.float32),
+            pltpu.VMEM((modes, CHUNKS, LANES), jnp.float32),
+            pltpu.VMEM((length, LANES), jnp.float32),
+        ],
+        compiler_params=pltpu.CompilerParams(vmem_limit_bytes=32 * 2**20),
+    )(rows, rows, rows, rate.T, mode_scale(rate).T, residue.T, carried.T)
+    return gated, state.T
+
+
+def per_device_channels(tokens, w_query, w_key, w_value, decay_rate, residue, carried):
+    gathered = lax.all_gather(tokens, ("chan", "rep"), axis=1, tiled=True)
+    gathered = lax.all_gather(gathered, "seq", axis=0, tiled=True)
+    weights = jnp.concatenate(
+        [
+            lax.all_to_all(w, "seq", split_axis=1, concat_axis=0, tiled=True)
+            for w in (w_query, w_key, w_value)
+        ],
+        axis=1,
+    )
+    rows = lax.dot_general(
+        gathered, weights, (((1,), (0,)), ((), ())), preferred_element_type=jnp.float32
+    ).astype(jnp.bfloat16)
+    gated, new_state = gated_scan(rows, decay_rate, residue, carried)
+    gated = lax.all_to_all(gated, "seq", split_axis=0, concat_axis=1, tiled=True)
+    return gated, new_state
+
+
 def solution(mesh):
     in_specs = (
         P(("parts", "seq"), ("chan", "rep")),
@@ -111,6 +228,10 @@
         P(("parts", "chan", "rep", "seq"), None),
     )
     out_specs = (P(("parts", "seq"), ("chan", "rep")), P(("parts", "chan", "rep", "seq"), None))
-    return jax.shard_map(
-        per_device, mesh=mesh, in_specs=in_specs, out_specs=out_specs, check_vma=False
-    )
+
+    def body(*arrays):
+        own_channels = arrays[4].shape[0]
+        chosen = per_device_channels if own_channels % LANES == 0 else per_device
+        return chosen(*arrays)
+
+    return jax.shard_map(body, mesh=mesh, in_specs=in_specs, out_specs=out_specs, check_vma=False)

time: 893 us -> 529 us (0.59)
  local copies, waits for them, and re-layouts: 337 us -> 22.4 us
  waiting for transfers between devices: 470 us -> 421 us
  matrix products: 50.3 us -> 17.5 us
  blocking collectives: 0 us -> 28.6 us
  other arithmetic: 12 us -> 0.02 us
  Pallas kernels: 0 us -> 11.9 us
    all_gather x4 -> x2, waiting for transfers between devices: 467 us -> 115 us  [the longest x1 76 us: per_device_channels(): gathered = lax.all_gather(gathered, 'seq', axis=0, tiled=True)]
    all_to_all x2 -> x3, waiting for transfers between devices: 0.01 us -> 305 us  [per_device_channels(): lax.all_to_all(w, 'seq', split_axis=1, concat_axis=0, tiled=True)]
    pad x6 -> x0, local copies, waits for them, and re-layouts: 158 us -> none  [block_sums(): lax.associative_scan(combine_states, (step_decay, block_ends), axis=1)]
    gather x2 -> x0, local copies, waits for them, and re-layouts: 80 us -> none  [block_convolve(): toeplitz = kernel[:, lag] * causal[None, :, :]]
    unnamed x33 -> x13, local copies, waits for them, and re-layouts: 82.2 us -> 10.8 us
    dot_general x6 -> x1, matrix products: 50.3 us -> 17.5 us  [per_device_channels(): lax.dot_general(gathered, weights, (((1,), (0,)), ((), ())), preferred_el...]
    all_to_all x0 -> x1, blocking collectives: none -> 28.6 us  [per_device_channels(): lax.all_to_all(gated, 'seq', split_axis=0, concat_axis=1, tiled=True)]
    slice x6 -> x0, local copies, waits for them, and re-layouts: 13.1 us -> none  [the longest x5 11.8 us: block_sums(): lax.associative_scan(combine_states, (step_decay, block_ends), axis=1)]
  transfers between devices with their start and end apart: 6 -> 5, of which waited for: 4 -> 5; matrix products, arithmetic and copies ran while one was open for 21% -> 4% of each run, Pallas kernels for 0% -> 0%
where the time goes in v1:
time: 529 us
  waiting for transfers between devices  421 us (80%)
  blocking collectives  28.6 us (5%)
  local copies, waits for them, and re-layouts  22.4 us (4%)
  matrix products  17.5 us (3%)
  between operations  14.1 us (3%)
  starting transfers between devices  13.6 us (3%)
  Pallas kernels  11.9 us (2%)
    all_to_all x3, waiting for transfers between devices, per_device_channels(): lax.all_to_all(w, 'seq', split_axis=1, concat_axis=0, tiled=True)  305 us
    all_gather x1, waiting for transfers between devices, per_device_channels(): gathered = lax.all_gather(gathered, 'seq', axis=0, tiled=True)  76 us
    all_gather x1, waiting for transfers between devices, per_device_channels(): gathered = lax.all_gather(tokens, ('chan', 'rep'), axis=1, tiled=True)  38.8 us
    all_to_all x1, blocking collectives, per_device_channels(): lax.all_to_all(gated, 'seq', split_axis=0, concat_axis=1, tiled=True)  28.6 us
    dot_general x1, matrix products, per_device_channels(): lax.dot_general(gathered, weights, (((1,), (0,)), ((), ())), preferred_el...  17.5 us
    all_to_all x3, starting transfers between devices, per_device_channels(): lax.all_to_all(w, 'seq', split_axis=1, concat_axis=0, tiled=True)  13.6 us
    pallas_call x1, Pallas kernels, gated_scan(): pl.pallas_call(scan_kernel, grid=(1,), out_shape=(jax.ShapeDtypeStruct((l...  11.9 us
    unnamed x13, local copies, waits for them, and re-layouts  10.8 us
  transfers between devices with their start and end apart: 5, of which 5 were waited for; matrix products, arithmetic and copies ran while one was open for 4% of the time, Pallas kernels for 0%

profile of v1, /device:TPU:0, one launch (start us, length us, event | category | flops | bytes accessed | tf_op | source)
XLA Modules:
  0.0 528.7 jit_solution(18055572152658904044)
XLA Ops:
  7.2 0.0 copy-start.3
  7.2 0.0 all-gather.3.cloned.1.call-start
  7.2 0.7 all-gather.3.cloned.1.call-update
  7.9 0.0 all-gather.5.cloned.1.call-start
  8.0 38.8 %all-gather.3.cloned.1.call-done = bf16[512,4096]{1,0:T(8,128)(2,1)} async-done(((bf16[512,1024]{1,0:T(8,128)(2,1)}), bf16[512,4096]{1,0:T(8,128)(2,1)}) %all-gather.3.cloned.1.call-update) | async-done | bytes 4194320 | tf_op jit(solution)/shard_map/all_gather | solution.py:203
  46.8 0.0 all-gather.5.cloned.1.call-update
  46.8 0.0 copy-done.3
  46.8 2.6 copy.17
  49.4 4.6 all-to-all-start.2
  54.0 4.2 copy.15
  58.2 100.8 %all-to-all-done.2 = bf16[1024,4,256]{0,2,1:T(8,128)(2,1)S(1)} async-done(((bf16[1024,4,256]{0,2,1:T(8,128)(2,1)}), bf16[1024,4,256]{0,2,1:T(8,128)(2,1)S(1)}, u32[]{:S(2)}, u32[]{:S(2)}) %all-to-all-start.2) | async-done | bytes 2097184 | tf_op jit(solution)/shard_map/all_to_all | solution.py:207
  158.9 4.5 all-to-all-start.1
  163.4 4.0 copy.13
  167.4 0.0 copy-start
  167.4 105.2 %all-to-all-done.1 = bf16[1024,4,256]{0,2,1:T(8,128)(2,1)} async-done(((bf16[1024,4,256]{0,2,1:T(8,128)(2,1)}), bf16[1024,4,256]{0,2,1:T(8,128)(2,1)}, u32[]{:S(2)}, u32[]{:S(2)}) %all-to-all-start.1) | async-done | bytes 2097184 | tf_op jit(solution)/shard_map/all_to_all | solution.py:207
  272.6 4.5 all-to-all-start
  277.1 0.0 copy-done
  277.2 2.6 copy.18
  279.8 4.0 copy.16
  283.7 0.0 copy-start.4
  283.7 99.0 %all-to-all-done = bf16[1024,4,256]{0,2,1:T(8,128)(2,1)} async-done(((bf16[1024,4,256]{0,2,1:T(8,128)(2,1)}), bf16[1024,4,256]{0,2,1:T(8,128)(2,1)}, u32[]{:S(2)}, u32[]{:S(2)}) %all-to-all-start) | async-done | bytes 2097184 | tf_op jit(solution)/shard_map/all_to_all | solution.py:207
  382.7 3.9 copy.14
  386.6 76.0 %all-gather.5.cloned.1.call-done = bf16[2048,4096]{1,0:T(8,128)(2,1)} async-done(((bf16[512,4096]{1,0:T(8,128)(2,1)}), bf16[2048,4096]{1,0:T(8,128)(2,1)}) %all-gather.5.cloned.1.call-update) | async-done | bytes 16777232 | tf_op jit(solution)/shard_map/all_gather | solution.py:204
  462.7 0.0 copy-done.4
  462.7 0.0 copy-start.1
  462.7 0.0 copy-start.2
  462.7 17.5 %fusion.9.q_ref.k_ref.v_ref = bf16[2048,768]{1,0:T(8,128)(2,1)S(1)} fusion(bf16[2048,4096]{1,0:T(8,128)(2,1)} %all-gather.5.cloned.1.call-done, bf16[4096,256]{1,0:T(8,128)(2,1)S(1)} %bitcast.31, bf16[4096,256]{1,0:T(8,128)(2,1)} %bitcast.32, bf16[4096,256]{1,0:T(8,128)(2,1)} %bitcast.33), kind=kOutput, calls=%fused_computation.7 | convolution fusion | flops 12905349120 | bytes 26214400 | tf_op jit(solution)/shard_map/dot_general | solution.py:212
  480.2 0.0 copy-done.1
  480.2 0.0 copy-done.2
  480.2 11.9 %shard_map.86 = (bf16[2048,256]{1,0:T(8,128)(2,1)S(1)}, f32[16,256]{1,0:T(8,128)}) custom-call(bf16[2048,768]{1,0:T(8,128)(2,1)S(1)} %fusion.9.q_ref.k_ref.v_ref, bf16[2048,768]{1,0:T(8,128)(2,1)S(1)} %fusion.9.q_ref.k_ref.v_ref, bf16[2048,768]{1,0:T(8,128)(2,1)S(1)} %fusion.9.q_ref.k_ref.v_ref, f32[16,256]{1,0:T(8,128)S(1)} %bitcast.23, ...), custom_call_target="tpu_custom_call" | custom-call | tf_op jit(solution)/shard_map/pallas_call | solution.py:181
  492.1 28.6 %all_to_all.76 = bf16[4,512,256]{2,1,0:T(8,128)(2,1)S(1)} all-to-all(bf16[4,512,256]{2,1,0:T(8,128)(2,1)S(1)} %bitcast.22), channel_id=1, replica_groups=mesh['parts'=2,'seq'=4,'chan'=2,'rep'=2] {'seq'}, dimensions={0} | all-to-all | bytes 2097152 | tf_op jit(solution)/shard_map/all_to_all | solution.py:216
  520.7 1.1 copy.22
  (1 shorter events, 0.0 us)
Async XLA Ops:
  7.2 39.6 %copy-start.3 = (bf16[1024,1024]{1,0:T(8,128)(2,1)S(1)}, bf16[1024,1024]{1,0:T(8,128)(2,1)}, u32[]{:S(2)}) copy-start(bf16[1024,1024]{1,0:T(8,128)(2,1)} %param.10) | copy-start | bytes 6291460
  7.2 39.6 %all-gather.3.cloned.1.call-start = ((), (), s32[]{:S(2)}) async-start(), calls=%async_computation.4 | async-start | bytes 5242880 | tf_op jit(solution)/shard_map/all_gather | solution.py:203
  7.9 454.8 %all-gather.5.cloned.1.call-start = ((), (), s32[]{:S(2)}) async-start(), calls=%async_computation.5 | async-start | bytes 20971520 | tf_op jit(solution)/shard_map/all_gather | solution.py:204
  49.4 109.5 %all-to-all-start.2 = ((bf16[1024,4,256]{0,2,1:T(8,128)(2,1)}), bf16[1024,4,256]{0,2,1:T(8,128)(2,1)S(1)}, u32[]{:S(2)}, u32[]{:S(2)}) async-start(bf16[1024,4,256]{0,2,1:T(8,128)(2,1)} %bitcast.29), calls=%async_computation.2 | async-start | bytes 4194304 | tf_op jit(solution)/shard_map/all_to_all | solution.py:207
  158.9 113.7 %all-to-all-start.1 = ((bf16[1024,4,256]{0,2,1:T(8,128)(2,1)}), bf16[1024,4,256]{0,2,1:T(8,128)(2,1)}, u32[]{:S(2)}, u32[]{:S(2)}) async-start(bf16[1024,4,256]{0,2,1:T(8,128)(2,1)} %bitcast.28), calls=%async_computation.1 | async-start | bytes 4194304 | tf_op jit(solution)/shard_map/all_to_all | solution.py:207
  167.4 109.8 %copy-start = (f32[256,16]{0,1:T(8,128)S(1)}, f32[256,16]{0,1:T(8,128)}, u32[]{:S(2)}) copy-start(f32[256,16]{0,1:T(8,128)} %param.11) | copy-start | bytes 49156
  272.6 110.1 %all-to-all-start = ((bf16[1024,4,256]{0,2,1:T(8,128)(2,1)}), bf16[1024,4,256]{0,2,1:T(8,128)(2,1)}, u32[]{:S(2)}, u32[]{:S(2)}) async-start(bf16[1024,4,256]{0,2,1:T(8,128)(2,1)} %bitcast.27), calls=%async_computation | async-start | bytes 4194304 | tf_op jit(solution)/shard_map/all_to_all | solution.py:207
  283.7 179.0 %copy-start.4 = (bf16[4,1024,256]{2,1,0:T(8,128)(2,1)S(1)}, bf16[4,1024,256]{2,1,0:T(8,128)(2,1)}, u32[]{:S(2)}) copy-start(bf16[4,1024,256]{2,1,0:T(8,128)(2,1)} %copy.18) | copy-start | bytes 6291460
  462.7 17.5 %copy-start.1 = (f32[256,16]{0,1:T(8,128)S(1)}, f32[256,16]{0,1:T(8,128)}, u32[]{:S(2)}) copy-start(f32[256,16]{0,1:T(8,128)} %param.12) | copy-start | bytes 49156
  462.7 17.5 %copy-start.2 = (f32[256,16]{0,1:T(8,128)S(1)}, f32[256,16]{0,1:T(8,128)}, u32[]{:S(2)}) copy-start(f32[256,16]{0,1:T(8,128)} %param.13) | copy-start | bytes 49156
Sparse Core Ops, SparseCore 0:
  9.5 37.1 all-gather.2
  48.3 414.3 all-gather.4

commit v2 on v1

--- a/solution.py
+++ b/solution.py
@@ -199,16 +199,234 @@
     return gated, state.T
 
 
+MESH = pl.DeviceIdType.MESH
+PIECES = 2
+
+
+def gather_kernel(count, tokens_ref, query_ref, key_ref, value_ref, all_ref, weights_ref,
+                  tokens_vmem, weights_vmem, local_sem, fill_sem,
+                  hop_send, hop_recv, side_send, side_recv, core_send, core_recv,
+                  part_send, part_recv, layer_send, layer_recv):
+    part, seq, chan, rep = (lax.axis_index(a) for a in ("parts", "seq", "chan", "rep"))
+    rows, columns = tokens_ref.shape
+    depth, outer = query_ref.shape
+    width = outer // count
+    half = depth // 2
+    piece = rows // PIECES
+    matrices = (query_ref, key_ref, value_ref)
+
+    barrier = pltpu.get_barrier_semaphore()
+    mates = ({"parts": 1 - part}, {"chan": 1 - chan}, {"rep": 1 - rep})
+    for mate in mates:
+        pl.semaphore_signal(barrier, inc=1, device_id=mate, device_id_type=MESH)
+    for step in range(1, count):
+        pl.semaphore_signal(
+            barrier, inc=1, device_id={"seq": lax.rem(seq + step, count)}, device_id_type=MESH
+        )
+    pl.semaphore_wait(barrier, count - 1 + len(mates))
+
+    def token_block(block, side, core, p):
+        top = pl.multiple_of(block * rows + p * piece, piece)
+        left = pl.multiple_of((side * 2 + core) * columns, columns)
+        return all_ref.at[pl.ds(top, piece), pl.ds(left, columns)]
+
+    def own_piece(p):
+        return tokens_ref.at[pl.ds(p * piece, piece), :]
+
+    def remote(source, target, send, recv, device):
+        return pltpu.make_async_remote_copy(
+            src_ref=source, dst_ref=target, send_sem=send, recv_sem=recv,
+            device_id=device, device_id_type=MESH,
+        )
+
+    def hop(block, p, way, source=None):
+        here = token_block(block, chan, rep, p)
+        device = {"seq": seq + 1 if way == 0 else seq - 1}
+        return remote(here if source is None else source, here, hop_send.at[block, p, way], hop_recv.at[block, p], device)
+
+    def side(block, p, source=None):
+        here = token_block(block, chan, rep, p)
+        return remote(here if source is None else source, here, side_send.at[block, p], side_recv.at[block, p], {"chan": 1 - chan})
+
+    def side_arrival(block, p):
+        there = token_block(block, 1 - chan, rep, p)
+        return remote(there, there, side_send.at[block, p], side_recv.at[block, p], {"chan": 1 - chan})
+
+    def core(block, which, p, source=None):
+        here = token_block(block, chan if which == 0 else 1 - chan, rep, p)
+        return remote(here if source is None else source, here, core_send.at[block, which, p], core_recv.at[block, which, p], {"rep": 1 - rep})
+
+    def core_arrival(block, which, p):
+        there = token_block(block, chan if which == 0 else 1 - chan, 1 - rep, p)
+        return remote(there, there, core_send.at[block, which, p], core_recv.at[block, which, p], {"rep": 1 - rep})
+
+    def weight_block(block, m, part_of):
+        top = pl.multiple_of(block * depth + part_of * half, half)
+        return weights_ref.at[pl.ds(top, half), pl.ds(m * width, width)]
+
+    def spread(target, m):
+        source = matrices[m].at[
+            pl.ds(pl.multiple_of(part * half, half), half),
+            pl.ds(pl.multiple_of(target * width, width), width),
+        ]
+        return remote(source, weight_block(seq, m, part), layer_send.at[target, m], layer_recv.at[seq, m], {"seq": target})
+
+    def spread_arrival(block, m):
+        here = weight_block(block, m, part)
+        return remote(here, here, layer_send.at[block, m], layer_recv.at[block, m], {"seq": block})
+
+    def swap(block, m):
+        here = weight_block(block, m, part)
+        return remote(here, here, part_send.at[block, m], part_recv.at[block, m], {"parts": 1 - part})
+
+    def swap_arrival(block, m):
+        there = weight_block(block, m, 1 - part)
+        return remote(there, there, part_send.at[block, m], part_recv.at[block, m], {"parts": 1 - part})
+
+    def sources(distance):
+        return ((seq >= distance, seq - distance, 0), (seq + distance < count, seq + distance, 1))
+
+    def has_next(way):
+        return seq + 1 < count if way == 0 else seq >= 1
+
+    def send_weights(distance):
+        for there, other, _ in sources(distance):
+            @pl.when(there)
+            def _():
+                for m in range(3):
+                    spread(other, m).start()
+
+    fills = [pltpu.make_async_copy(tokens_ref, tokens_vmem, fill_sem.at[3])] + [
+        pltpu.make_async_copy(
+            matrices[m].at[:, pl.ds(pl.multiple_of(seq * width, width), width)],
+            weights_vmem.at[:, pl.ds(m * width, width)], fill_sem.at[m])
+        for m in range(3)
+    ]
+    for p in range(PIECES):
+        for way in range(2):
+            @pl.when(has_next(way))
+            def _():
+                hop(seq, p, way, own_piece(p)).start()
+        side(seq, p, own_piece(p)).start()
+        core(seq, 0, p, own_piece(p)).start()
+    send_weights(1)
+    for fill in fills:
+        fill.start()
+    for fill in fills:
+        fill.wait()
+    locals_ = [
+        pltpu.make_async_copy(
+            tokens_vmem,
+            all_ref.at[pl.ds(pl.multiple_of(seq * rows, rows), rows),
+                       pl.ds(pl.multiple_of((chan * 2 + rep) * columns, columns), columns)],
+            local_sem.at[0]),
+        pltpu.make_async_copy(
+            weights_vmem, weights_ref.at[pl.ds(pl.multiple_of(seq * depth, depth), depth), :],
+            local_sem.at[1]),
+    ]
+    for copy in locals_:
+        copy.start()
+
+    def pass_side(block):
+        for p in range(PIECES):
+            side_arrival(block, p).wait_recv()
+            core(block, 1, p).start()
+
+    for distance in range(1, count):
+        for p in range(PIECES):
+            for there, other, way in sources(distance):
+                @pl.when(there)
+                def _():
+                    hop(other, p, way).wait_recv()
+
+                    @pl.when(has_next(way))
+                    def _():
+                        hop(other, p, way).start()
+
+                    side(other, p).start()
+                    core(other, 0, p).start()
+        if distance + 1 < count:
+            send_weights(distance + 1)
+        for m in range(3):
+            for there, other, _ in sources(distance):
+                @pl.when(there)
+                def _():
+                    spread_arrival(other, m).wait_recv()
+                    swap(other, m).start()
+        if distance == 1:
+            pass_side(seq)
+        else:
+            for there, other, _ in sources(distance - 1):
+                @pl.when(there)
+                def _():
+                    pass_side(other)
+    for there, other, _ in sources(count - 1):
+        @pl.when(there)
+        def _():
+            pass_side(other)
+
+    for copy in locals_:
+        copy.wait()
+    for p in range(PIECES):
+        for way in range(2):
+            @pl.when(has_next(way))
+            def _():
+                hop(seq, p, way, own_piece(p)).wait_send()
+        side(seq, p, own_piece(p)).wait_send()
+        core(seq, 0, p, own_piece(p)).wait_send()
+        core(seq, 1, p).wait_send()
+        for which in range(2):
+            core_arrival(seq, which, p).wait_recv()
+    for distance in range(1, count):
+        for there, other, way in sources(distance):
+            @pl.when(there)
+            def _():
+                for p in range(PIECES):
+                    @pl.when(has_next(way))
+                    def _():
+                        hop(other, p, way).wait_send()
+
+                    side(other, p).wait_send()
+                    for which in range(2):
+                        core(other, which, p).wait_send()
+                        core_arrival(other, which, p).wait_recv()
+                for m in range(3):
+                    spread(other, m).wait_send()
+                    swap(other, m).wait_send()
+                    swap_arrival(other, m).wait_recv()
+
+
+def gather(tokens, w_query, w_key, w_value, count):
+    rows, columns = tokens.shape
+    depth, outer = w_query.shape
+    width = outer // count
+    anywhere = pl.BlockSpec(memory_space=pl.ANY)
+    dma = pltpu.SemaphoreType.DMA
+    return pl.pallas_call(
+        functools.partial(gather_kernel, count),
+        out_shape=(
+            jax.ShapeDtypeStruct((rows * count, columns * 4), jnp.bfloat16),
+            jax.ShapeDtypeStruct((depth * count, width * 3), jnp.bfloat16),
+        ),
+        in_specs=[anywhere] * 4,
+        out_specs=(anywhere, anywhere),
+        scratch_shapes=[
+            pltpu.VMEM((rows, columns), jnp.bfloat16),
+            pltpu.VMEM((depth, width * 3), jnp.bfloat16),
+            dma((2,)), dma((4,)),
+            dma((count, PIECES, 2)), dma((count, PIECES)),
+            dma((count, PIECES)), dma((count, PIECES)),
+            dma((count, 2, PIECES)), dma((count, 2, PIECES)),
+            dma((count, 3)), dma((count, 3)),
+            dma((count, 3)), dma((count, 3)),
+        ],
+        compiler_params=pltpu.CompilerParams(collective_id=0, has_side_effects=True),
+    )(tokens, w_query, w_key, w_value)
+
+
 def per_device_channels(tokens, w_query, w_key, w_value, decay_rate, residue, carried):
-    gathered = lax.all_gather(tokens, ("chan", "rep"), axis=1, tiled=True)
-    gathered = lax.all_gather(gathered, "seq", axis=0, tiled=True)
-    weights = jnp.concatenate(
-        [
-            lax.all_to_all(w, "seq", split_axis=1, concat_axis=0, tiled=True)
-            for w in (w_query, w_key, w_value)
-        ],
-        axis=1,
-    )
+    count = lax.axis_size("seq")
+    gathered, weights = gather(tokens, w_query, w_key, w_value, count)
     rows = lax.dot_general(
         gathered, weights, (((1,), (0,)), ((), ())), preferred_element_type=jnp.float32
     ).astype(jnp.bfloat16)
@@ -231,7 +449,8 @@
 
     def body(*arrays):
         own_channels = arrays[4].shape[0]
-        chosen = per_device_channels if own_channels % LANES == 0 else per_device
+        mates = all(mesh.shape[a] == 2 for a in ("parts", "chan", "rep"))
+        chosen = per_device_channels if own_channels % LANES == 0 and mates else per_device
         return chosen(*arrays)
 
     return jax.shard_map(body, mesh=mesh, in_specs=in_specs, out_specs=out_specs, check_vma=False)

time: 529 us -> 211 us (0.40)
  waiting for transfers between devices: 421 us -> 0 us
  Pallas kernels: 11.9 us -> 163 us
  local copies, waits for them, and re-layouts: 22.4 us -> 1.13 us
  starting transfers between devices: 13.6 us -> 0 us
  between operations: 14.1 us -> 0.7 us
    all_to_all x3 -> x0, waiting for transfers between devices: 305 us -> none  [per_device_channels(): lax.all_to_all(w, 'seq', split_axis=1, concat_axis=0, tiled=True)]
    pallas_call x0 -> x1, Pallas kernels: none -> 151 us  [gather(): pl.pallas_call(functools.partial(gather_kernel, count), out_shape=(jax.Sh...]
    all_gather x2 -> x0, waiting for transfers between devices: 115 us -> none  [the longest x1 76 us: per_device_channels(): gathered = lax.all_gather(gathered, 'seq', axis=0, tiled=True)]
    all_to_all x3 -> x0, starting transfers between devices: 13.6 us -> none  [per_device_channels(): lax.all_to_all(w, 'seq', split_axis=1, concat_axis=0, tiled=True)]
    unnamed x13 -> x6, local copies, waits for them, and re-layouts: 10.8 us -> 0.02 us
    all_to_all x3 -> x0, local copies, waits for them, and re-layouts: 10.5 us -> none  [per_device_channels(): lax.all_to_all(w, 'seq', split_axis=1, concat_axis=0, tiled=True)]
  transfers between devices with their start and end apart: 5 -> 0, of which waited for: 5 -> 0; matrix products, arithmetic and copies ran while one was open for 4% -> 0% of each run, Pallas kernels for 0% -> 0%
where the time goes in v2:
time: 211 us
  Pallas kernels  163 us (77%)
  blocking collectives  27.9 us (13%)
  matrix products  18.1 us (9%)
    pallas_call x1, Pallas kernels, gather(): pl.pallas_call(functools.partial(gather_kernel, count), out_shape=(jax.Sh...  151 us
    all_to_all x1, blocking collectives, per_device_channels(): lax.all_to_all(gated, 'seq', split_axis=0, concat_axis=1, tiled=True)  27.9 us
    dot_general x1, matrix products, per_device_channels(): lax.dot_general(gathered, weights, (((1,), (0,)), ((), ())), preferred_el...  18.1 us
    pallas_call x1, Pallas kernels, gated_scan(): pl.pallas_call(scan_kernel, grid=(1,), out_shape=(jax.ShapeDtypeStruct((l...  11.9 us

profile of v2, /device:TPU:0, one launch (start us, length us, event | category | flops | bytes accessed | tf_op | source)
XLA Modules:
  0.0 211.1 jit_solution(7944829375567962171)
XLA Ops:
  0.6 0.7 sqrt_bitcast_fusion.scale_ref
  1.4 150.6 %shard_map.86 = (bf16[2048,4096]{1,0:T(8,128)(2,1)}, bf16[4096,768]{1,0:T(8,128)(2,1)}) custom-call(bf16[512,1024]{1,0:T(8,128)(2,1)} %tokens_ref.1, bf16[1024,1024]{1,0:T(8,128)(2,1)} %query_ref.1, bf16[1024,1024]{1,0:T(8,128)(2,1)} %key_ref.1, bf16[1024,1024]{1,0:T(8,128)(2,1)} %value_ref.1), custom_call_target="tpu_custom_call" | custom-call | tf_op jit(solution)/shard_map/pallas_call | solution.py:405
  152.0 0.0 copy-start
  152.0 0.0 copy-start.1
  152.1 0.0 copy-start.2
  152.1 18.1 %convolution_convert_fusion.q_ref.k_ref.v_ref = bf16[2048,768]{1,0:T(8,128)(2,1)S(1)} fusion(bf16[2048,4096]{1,0:T(8,128)(2,1)} %get-tuple-element.6, bf16[4096,768]{1,0:T(8,128)(2,1)} %get-tuple-element.7), kind=kOutput, calls=%fused_computation | convolution fusion | flops 12886474752 | bytes 26214400 | tf_op jit(solution)/shard_map/dot_general | solution.py:430
  170.1 0.0 copy-done
  170.1 0.0 copy-done.1
  170.2 0.0 copy-done.2
  170.2 11.9 %shard_map.87 = (bf16[2048,256]{1,0:T(8,128)(2,1)S(1)}, f32[16,256]{1,0:T(8,128)}) custom-call(bf16[2048,768]{1,0:T(8,128)(2,1)S(1)} %convolution_convert_fusion.q_ref.k_ref.v_ref, bf16[2048,768]{1,0:T(8,128)(2,1)S(1)} %convolution_convert_fusion.q_ref.k_ref.v_ref, bf16[2048,768]{1,0:T(8,128)(2,1)S(1)} %convolution_convert_fusion.q_ref.k_ref.v_ref, ...), custom_call_target="tpu_custom_call" | custom-call | tf_op jit(solution)/shard_map/pallas_call | solution.py:181
  182.1 27.9 %all_to_all.19 = bf16[4,512,256]{2,1,0:T(8,128)(2,1)S(1)} all-to-all(bf16[4,512,256]{2,1,0:T(8,128)(2,1)S(1)} %bitcast.12), channel_id=1, replica_groups=mesh['parts'=2,'seq'=4,'chan'=2,'rep'=2] {'seq'}, dimensions={0} | all-to-all | bytes 2097152 | tf_op jit(solution)/shard_map/all_to_all | solution.py:434
  210.0 1.1 copy.10
Async XLA Ops:
  152.0 18.1 %copy-start = (f32[256,16]{0,1:T(8,128)S(1)}, f32[256,16]{0,1:T(8,128)}, u32[]{:S(2)}) copy-start(f32[256,16]{0,1:T(8,128)} %param.11) | copy-start | bytes 49156
  152.0 18.1 %copy-start.1 = (f32[256,16]{0,1:T(8,128)S(1)}, f32[256,16]{0,1:T(8,128)}, u32[]{:S(2)}) copy-start(f32[256,16]{0,1:T(8,128)} %param.12) | copy-start | bytes 49156
  152.1 18.1 %copy-start.2 = (f32[256,16]{0,1:T(8,128)S(1)}, f32[256,16]{0,1:T(8,128)}, u32[]{:S(2)}) copy-start(f32[256,16]{0,1:T(8,128)} %param.13) | copy-start | bytes 49156

commit v3 on v2

--- a/solution.py
+++ b/solution.py
@@ -175,7 +175,7 @@
 
 
 def gated_scan(rows, rate, residue, carried):
-    length = rows.shape[0]
+    length = rows.shape[1]
     width, modes = rate.shape
     vmem = pl.BlockSpec(memory_space=pltpu.VMEM)
     gated, state = pl.pallas_call(
@@ -185,7 +185,7 @@
             jax.ShapeDtypeStruct((length, width), jnp.bfloat16),
             jax.ShapeDtypeStruct((modes, width), jnp.float32),
         ),
-        in_specs=[pl.BlockSpec((length, width), functools.partial(lambda j, i: (0, j), j)) for j in range(3)]
+        in_specs=[pl.BlockSpec((None, length, width), functools.partial(lambda j, i: (j, 0, 0), j)) for j in range(3)]
         + [vmem] * 4,
         out_specs=(pl.BlockSpec((length, width), lambda i: (0, 0)), vmem),
         scratch_shapes=[
@@ -203,8 +203,8 @@
 PIECES = 2
 
 
-def gather_kernel(count, tokens_ref, query_ref, key_ref, value_ref, all_ref, weights_ref,
-                  tokens_vmem, weights_vmem, local_sem, fill_sem,
+def project_kernel(count, tokens_ref, query_ref, key_ref, value_ref, out_ref,
+                   all_ref, weights_ref, fill_sem,
                   hop_send, hop_recv, side_send, side_recv, core_send, core_recv,
                   part_send, part_recv, layer_send, layer_recv):
     part, seq, chan, rep = (lax.axis_index(a) for a in ("parts", "seq", "chan", "rep"))
@@ -213,6 +213,7 @@
     width = outer // count
     half = depth // 2
     piece = rows // PIECES
+    own_columns = pl.ds(pl.multiple_of(seq * width, width), width)
     matrices = (query_ref, key_ref, value_ref)
 
     barrier = pltpu.get_barrier_semaphore()
@@ -262,7 +263,7 @@
 
     def weight_block(block, m, part_of):
         top = pl.multiple_of(block * depth + part_of * half, half)
-        return weights_ref.at[pl.ds(top, half), pl.ds(m * width, width)]
+        return weights_ref.at[m, pl.ds(top, half), :]
 
     def spread(target, m):
         source = matrices[m].at[
@@ -296,12 +297,32 @@
                 for m in range(3):
                     spread(other, m).start()
 
-    fills = [pltpu.make_async_copy(tokens_ref, tokens_vmem, fill_sem.at[3])] + [
+    def project(block):
+        top = pl.multiple_of(block * rows, rows)
+
+        def one(m, _):
+            out_ref[m, pl.ds(top, rows), :] = jnp.dot(
+                all_ref[pl.ds(top, rows), :], weights_ref[m], preferred_element_type=jnp.float32
+            ).astype(jnp.bfloat16)
+            return 0
+
+        lax.fori_loop(0, 3, one, 0)
+
+    fills = [
         pltpu.make_async_copy(
-            matrices[m].at[:, pl.ds(pl.multiple_of(seq * width, width), width)],
-            weights_vmem.at[:, pl.ds(m * width, width)], fill_sem.at[m])
+            tokens_ref,
+            all_ref.at[pl.ds(pl.multiple_of(seq * rows, rows), rows),
+                       pl.ds(pl.multiple_of((chan * 2 + rep) * columns, columns), columns)],
+            fill_sem.at[3])
+    ] + [
+        pltpu.make_async_copy(
+            matrices[m].at[:, own_columns],
+            weights_ref.at[m, pl.ds(pl.multiple_of(seq * depth, depth), depth), :],
+            fill_sem.at[m])
         for m in range(3)
     ]
+    for distance in range(1, count):
+        send_weights(distance)
     for p in range(PIECES):
         for way in range(2):
             @pl.when(has_next(way))
@@ -309,28 +330,41 @@
                 hop(seq, p, way, own_piece(p)).start()
         side(seq, p, own_piece(p)).start()
         core(seq, 0, p, own_piece(p)).start()
-    send_weights(1)
     for fill in fills:
         fill.start()
-    for fill in fills:
-        fill.wait()
-    locals_ = [
-        pltpu.make_async_copy(
-            tokens_vmem,
-            all_ref.at[pl.ds(pl.multiple_of(seq * rows, rows), rows),
-                       pl.ds(pl.multiple_of((chan * 2 + rep) * columns, columns), columns)],
-            local_sem.at[0]),
-        pltpu.make_async_copy(
-            weights_vmem, weights_ref.at[pl.ds(pl.multiple_of(seq * depth, depth), depth), :],
-            local_sem.at[1]),
-    ]
-    for copy in locals_:
-        copy.start()
 
     def pass_side(block):
         for p in range(PIECES):
             side_arrival(block, p).wait_recv()
             core(block, 1, p).start()
+
+    pass_side(seq)
+    for distance in range(1, count):
+        for m in range(3):
+            for there, other, _ in sources(distance):
+                @pl.when(there)
+                def _():
+                    spread_arrival(other, m).wait_recv()
+                    swap(other, m).start()
+    for fill in fills:
+        fill.wait()
+
+    def core_arrivals(block):
+        for p in range(PIECES):
+            for which in range(2):
+                core_arrival(block, which, p).wait_recv()
+
+    def finish(distance):
+        if distance == 0:
+            core_arrivals(seq)
+            project(seq)
+        else:
+            for there, other, _ in sources(distance):
+                @pl.when(there)
+                def _():
+                    pass_side(other)
+                    core_arrivals(other)
+                    project(other)
 
     for distance in range(1, count):
         for p in range(PIECES):
@@ -345,28 +379,15 @@
 
                     side(other, p).start()
                     core(other, 0, p).start()
-        if distance + 1 < count:
-            send_weights(distance + 1)
-        for m in range(3):
-            for there, other, _ in sources(distance):
+        if distance == 1:
+            for there, other, _ in [s for d in range(1, count) for s in sources(d)]:
                 @pl.when(there)
                 def _():
-                    spread_arrival(other, m).wait_recv()
-                    swap(other, m).start()
-        if distance == 1:
-            pass_side(seq)
-        else:
-            for there, other, _ in sources(distance - 1):
-                @pl.when(there)
-                def _():
-                    pass_side(other)
-    for there, other, _ in sources(count - 1):
-        @pl.when(there)
-        def _():
-            pass_side(other)
-
-    for copy in locals_:
-        copy.wait()
+                    for m in range(3):
+                        swap_arrival(other, m).wait_recv()
+        finish(distance - 1)
+    finish(count - 1)
+
     for p in range(PIECES):
         for way in range(2):
             @pl.when(has_next(way))
@@ -375,8 +396,6 @@
         side(seq, p, own_piece(p)).wait_send()
         core(seq, 0, p, own_piece(p)).wait_send()
         core(seq, 1, p).wait_send()
-        for which in range(2):
-            core_arrival(seq, which, p).wait_recv()
     for distance in range(1, count):
         for there, other, way in sources(distance):
             @pl.when(there)
@@ -389,47 +408,41 @@
                     side(other, p).wait_send()
                     for which in range(2):
                         core(other, which, p).wait_send()
-                        core_arrival(other, which, p).wait_recv()
                 for m in range(3):
                     spread(other, m).wait_send()
                     swap(other, m).wait_send()
-                    swap_arrival(other, m).wait_recv()
-
-
-def gather(tokens, w_query, w_key, w_value, count):
+
+
+def project_all(tokens, w_query, w_key, w_value, count):
     rows, columns = tokens.shape
     depth, outer = w_query.shape
     width = outer // count
     anywhere = pl.BlockSpec(memory_space=pl.ANY)
     dma = pltpu.SemaphoreType.DMA
     return pl.pallas_call(
-        functools.partial(gather_kernel, count),
-        out_shape=(
-            jax.ShapeDtypeStruct((rows * count, columns * 4), jnp.bfloat16),
-            jax.ShapeDtypeStruct((depth * count, width * 3), jnp.bfloat16),
-        ),
+        functools.partial(project_kernel, count),
+        out_shape=jax.ShapeDtypeStruct((3, rows * count, width), jnp.bfloat16),
         in_specs=[anywhere] * 4,
-        out_specs=(anywhere, anywhere),
+        out_specs=pl.BlockSpec(memory_space=pltpu.VMEM),
         scratch_shapes=[
-            pltpu.VMEM((rows, columns), jnp.bfloat16),
-            pltpu.VMEM((depth, width * 3), jnp.bfloat16),
-            dma((2,)), dma((4,)),
+            pltpu.VMEM((rows * count, columns * 4), jnp.bfloat16),
+            pltpu.VMEM((3, depth * count, width), jnp.bfloat16),
+            dma((4,)),
             dma((count, PIECES, 2)), dma((count, PIECES)),
             dma((count, PIECES)), dma((count, PIECES)),
             dma((count, 2, PIECES)), dma((count, 2, PIECES)),
             dma((count, 3)), dma((count, 3)),
             dma((count, 3)), dma((count, 3)),
         ],
-        compiler_params=pltpu.CompilerParams(collective_id=0, has_side_effects=True),
+        compiler_params=pltpu.CompilerParams(
+            collective_id=0, has_side_effects=True, vmem_limit_bytes=50 * 2**20
+        ),
     )(tokens, w_query, w_key, w_value)
 
 
 def per_device_channels(tokens, w_query, w_key, w_value, decay_rate, residue, carried):
     count = lax.axis_size("seq")
-    gathered, weights = gather(tokens, w_query, w_key, w_value, count)
-    rows = lax.dot_general(
-        gathered, weights, (((1,), (0,)), ((), ())), preferred_element_type=jnp.float32
-    ).astype(jnp.bfloat16)
+    rows = project_all(tokens, w_query, w_key, w_value, count)
     gated, new_state = gated_scan(rows, decay_rate, residue, carried)
     gated = lax.all_to_all(gated, "seq", split_axis=0, concat_axis=1, tiled=True)
     return gated, new_state

time: 211 us -> 208 us (0.986)
  matrix products: 18.1 us -> 0 us
  blocking collectives: 27.9 us -> 36.7 us
  local copies, waits for them, and re-layouts: 1.13 us -> 5.82 us
    dot_general x1 -> x0, matrix products: 18.1 us -> none  [per_device_channels(): lax.dot_general(gathered, weights, (((1,), (0,)), ((), ())), preferred_el...]
    all_to_all x1, blocking collectives: 27.9 us -> 36.7 us  [per_device_channels(): lax.all_to_all(gated, 'seq', split_axis=0, concat_axis=1, tiled=True)]
    unnamed x6 -> x12, local copies, waits for them, and re-layouts: 0.02 us -> 4.7 us
where the time goes in v3:
time: 208 us
  Pallas kernels  164 us (79%)
  blocking collectives  36.7 us (18%)
  local copies, waits for them, and re-layouts  5.82 us (3%)
    pallas_call x1, Pallas kernels, project_all(): pl.pallas_call(functools.partial(project_kernel, count), out_shape=jax.Sh...  152 us
    all_to_all x1, blocking collectives, per_device_channels(): lax.all_to_all(gated, 'seq', split_axis=0, concat_axis=1, tiled=True)  36.7 us
    pallas_call x1, Pallas kernels, gated_scan(): pl.pallas_call(scan_kernel, grid=(1,), out_shape=(jax.ShapeDtypeStruct((l...  11.7 us
    unnamed x12, local copies, waits for them, and re-layouts  4.7 us

profile of v3, /device:TPU:0, one launch (start us, length us, event | category | flops | bytes accessed | tf_op | source)
XLA Modules:
  0.0 208.1 jit_solution(3478078997542771847)
XLA Ops:
  0.6 0.7 sqrt_bitcast_fusion.scale_ref
  1.4 0.0 copy-start.1
  1.4 1.6 copy-done.1
  3.0 0.0 copy-start.2
  3.0 1.2 copy-done.2
  4.2 0.0 copy-start.3
  4.2 0.0 copy-start.4
  4.2 0.0 copy-start.5
  4.2 152.4 %shard_map.86.q_ref.k_ref.v_ref = bf16[3,2048,256]{2,1,0:T(8,128)(2,1)} custom-call(bf16[512,1024]{1,0:T(8,128)(2,1)S(1)} %copy-done.2, bf16[1024,1024]{1,0:T(8,128)(2,1)S(1)} %copy-done.1, bf16[1024,1024]{1,0:T(8,128)(2,1)} %key_ref.1, bf16[1024,1024]{1,0:T(8,128)(2,1)} %value_ref.1), custom_call_target="tpu_custom_call" | custom-call | tf_op jit(solution)/shard_map/pallas_call | solution.py:422
  156.6 0.0 copy-done.3
  156.6 0.0 copy-done.4
  156.6 0.0 copy-done.5
  156.7 0.0 copy-start
  156.7 1.9 copy-done
  158.5 11.7 %shard_map.87 = (bf16[2048,256]{1,0:T(8,128)(2,1)S(1)}, f32[16,256]{1,0:T(8,128)}) custom-call(bf16[3,2048,256]{2,1,0:T(8,128)(2,1)S(1)} %copy-done, bf16[3,2048,256]{2,1,0:T(8,128)(2,1)S(1)} %copy-done, bf16[3,2048,256]{2,1,0:T(8,128)(2,1)S(1)} %copy-done, f32[16,256]{1,0:T(8,128)S(1)} %bitcast.11, f32[16,256]{1,0:T(8,128)S(1)} %sqrt_bitcast_fusion.scale_ref, ...), custom_call_target="tpu_custom_call" | custom-call | tf_op jit(solution)/shard_map/pallas_call | solution.py:181
  170.2 36.7 %all_to_all.19 = bf16[4,512,256]{2,1,0:T(8,128)(2,1)S(1)} all-to-all(bf16[4,512,256]{2,1,0:T(8,128)(2,1)S(1)} %bitcast.10), channel_id=1, replica_groups=mesh['parts'=2,'seq'=4,'chan'=2,'rep'=2] {'seq'}, dimensions={0} | all-to-all | bytes 2097152 | tf_op jit(solution)/shard_map/all_to_all | solution.py:447
  207.0 1.1 copy.10
Async XLA Ops:
  1.4 1.6 copy-start.1
  3.0 1.2 copy-start.2
  4.2 152.4 %copy-start.3 = (f32[256,16]{0,1:T(8,128)S(1)}, f32[256,16]{0,1:T(8,128)}, u32[]{:S(2)}) copy-start(f32[256,16]{0,1:T(8,128)} %param.11) | copy-start | bytes 49156
  4.2 152.4 %copy-start.4 = (f32[256,16]{0,1:T(8,128)S(1)}, f32[256,16]{0,1:T(8,128)}, u32[]{:S(2)}) copy-start(f32[256,16]{0,1:T(8,128)} %param.12) | copy-start | bytes 49156
  4.2 152.5 %copy-start.5 = (f32[256,16]{0,1:T(8,128)S(1)}, f32[256,16]{0,1:T(8,128)}, u32[]{:S(2)}) copy-start(f32[256,16]{0,1:T(8,128)} %param.13) | copy-start | bytes 49156
  156.7 1.9 copy-start

commit v4 on v3

--- a/solution.py
+++ b/solution.py
@@ -10,6 +10,7 @@
 BLOCK = 128
 LANES = 128
 CHUNKS = 8
+MESH = pl.DeviceIdType.MESH
 
 
 HIGHEST_PRECISION = lax.Precision.HIGHEST
@@ -106,9 +107,57 @@
     return (gated_rows.T, new_state)
 
 
-def scan_kernel(q_ref, k_ref, v_ref, rate_ref, scale_ref, residue_ref, carried_ref, gated_ref,
-                state_ref, signal, ends, entering, conv):
+def scan_kernel(count, q_ref, k_ref, v_ref, rate_hbm, scale_hbm, residue_hbm, carried_hbm, out_ref,
+                state_ref, rate_ref, scale_ref, residue_ref, carried_ref, signal, ends, entering, conv,
+                gated_ref, fill_sem, own_sem, send_sem, recv_sem):
+    seq = lax.axis_index("seq")
+    barrier = pltpu.get_barrier_semaphore()
+    for step in range(1, count):
+        pl.semaphore_signal(
+            barrier, inc=1, device_id={"seq": lax.rem(seq + step, count)}, device_id_type=MESH
+        )
+    fills = [
+        pltpu.make_async_copy(source, target, fill_sem.at[n])
+        for n, (source, target) in enumerate((
+            (rate_hbm, rate_ref), (scale_hbm, scale_ref),
+            (residue_hbm, residue_ref), (carried_hbm, carried_ref),
+        ))
+    ]
+    for fill in fills:
+        fill.start()
     length, width = q_ref.shape
+    rows_out = length // count
+
+    def columns_of(source, lane):
+        return out_ref.at[:, pl.ds(pl.multiple_of(source * width + lane, LANES), LANES)]
+
+    def block_of(target, lane):
+        top = pl.multiple_of(target * rows_out, rows_out)
+        return gated_ref.at[pl.ds(top, rows_out), pl.ds(lane, LANES)]
+
+    def give(step, lane):
+        target = lax.rem(seq + step, count)
+        group = lane // LANES
+        return pltpu.make_async_remote_copy(
+            src_ref=block_of(target, lane), dst_ref=columns_of(seq, lane),
+            send_sem=send_sem.at[target, group], recv_sem=recv_sem.at[seq, group],
+            device_id={"seq": target}, device_id_type=MESH,
+        )
+
+    def take(step, lane):
+        source = lax.rem(seq + step, count)
+        group = lane // LANES
+        return pltpu.make_async_remote_copy(
+            src_ref=columns_of(source, lane), dst_ref=columns_of(source, lane),
+            send_sem=send_sem.at[source, group], recv_sem=recv_sem.at[source, group],
+            device_id={"seq": source}, device_id_type=MESH,
+        )
+
+    def keep(lane):
+        return pltpu.make_async_copy(
+            block_of(seq, lane), columns_of(seq, lane), own_sem.at[lane // LANES]
+        )
+
     modes = rate_ref.shape[0]
     chunk = length // CHUNKS
     rows_at = 256
@@ -122,6 +171,9 @@
             return 0
 
         lax.fori_loop(0, length // rows_at, multiply, 0)
+        if lane == 0:
+            for fill in fills:
+                fill.wait()
         rates = rate_ref[:, lanes]
         residues = residue_ref[:, lanes]
         scale = scale_ref[:, lanes]
@@ -172,34 +224,51 @@
             return 0
 
         lax.fori_loop(0, length // rows_at, gate, 0)
-
-
-def gated_scan(rows, rate, residue, carried):
+        if lane == 0:
+            pl.semaphore_wait(barrier, count - 1)
+        for step in range(1, count):
+            give(step, lane).start()
+        keep(lane).start()
+    for lane in range(0, width, LANES):
+        keep(lane).wait()
+        for step in range(1, count):
+            take(step, lane).wait_recv()
+            give(step, lane).wait_send()
+
+
+def gated_scan(rows, rate, residue, carried, count):
     length = rows.shape[1]
     width, modes = rate.shape
     vmem = pl.BlockSpec(memory_space=pltpu.VMEM)
+    anywhere = pl.BlockSpec(memory_space=pl.ANY)
+    dma = pltpu.SemaphoreType.DMA
+    table = pltpu.VMEM((modes, width), jnp.float32)
     gated, state = pl.pallas_call(
-        scan_kernel,
+        functools.partial(scan_kernel, count),
         grid=(1,),
         out_shape=(
-            jax.ShapeDtypeStruct((length, width), jnp.bfloat16),
+            jax.ShapeDtypeStruct((length // count, width * count), jnp.bfloat16),
             jax.ShapeDtypeStruct((modes, width), jnp.float32),
         ),
         in_specs=[pl.BlockSpec((None, length, width), functools.partial(lambda j, i: (j, 0, 0), j)) for j in range(3)]
-        + [vmem] * 4,
-        out_specs=(pl.BlockSpec((length, width), lambda i: (0, 0)), vmem),
-        scratch_shapes=[
+        + [anywhere] * 4,
+        out_specs=(anywhere, vmem),
+        scratch_shapes=[table] * 4 + [
             pltpu.VMEM((length, LANES), jnp.float32),
             pltpu.VMEM((modes, CHUNKS, LANES), jnp.float32),
             pltpu.VMEM((modes, CHUNKS, LANES), jnp.float32),
             pltpu.VMEM((length, LANES), jnp.float32),
+            pltpu.VMEM((length, width), jnp.bfloat16),
+            dma((4,)), dma((width // LANES,)),
+            dma((count, width // LANES)), dma((count, width // LANES)),
         ],
-        compiler_params=pltpu.CompilerParams(vmem_limit_bytes=32 * 2**20),
+        compiler_params=pltpu.CompilerParams(
+            collective_id=1, has_side_effects=True, vmem_limit_bytes=32 * 2**20
+        ),
     )(rows, rows, rows, rate.T, mode_scale(rate).T, residue.T, carried.T)
     return gated, state.T
 
 
-MESH = pl.DeviceIdType.MESH
 PIECES = 2
 
 
@@ -443,9 +512,7 @@
 def per_device_channels(tokens, w_query, w_key, w_value, decay_rate, residue, carried):
     count = lax.axis_size("seq")
     rows = project_all(tokens, w_query, w_key, w_value, count)
-    gated, new_state = gated_scan(rows, decay_rate, residue, carried)
-    gated = lax.all_to_all(gated, "seq", split_axis=0, concat_axis=1, tiled=True)
-    return gated, new_state
+    return gated_scan(rows, decay_rate, residue, carried, count)
 
 
 def solution(mesh):

time: 208 us -> 193 us (0.928)
  blocking collectives: 36.7 us -> 0 us
  Pallas kernels: 164 us -> 184 us
    all_to_all x1 -> x0, blocking collectives: 36.7 us -> none  [per_device_channels(): lax.all_to_all(gated, 'seq', split_axis=0, concat_axis=1, tiled=True)]
    pallas_call x1, Pallas kernels: 11.7 us -> 31.8 us  [gated_scan(): pl.pallas_call(functools.partial(scan_kernel, count), grid=(1,), out_shap...]
    unnamed x12 -> x14, local copies, waits for them, and re-layouts: 4.7 us -> 6.28 us
where the time goes in v4:
time: 193 us; the launch traced here: 192 us
  Pallas kernels  184 us (95%)
  local copies, waits for them, and re-layouts  6.28 us (3%)
    pallas_call x1, Pallas kernels, project_all(): pl.pallas_call(functools.partial(project_kernel, count), out_shape=jax.Sh...  152 us
    pallas_call x1, Pallas kernels, gated_scan(): pl.pallas_call(functools.partial(scan_kernel, count), grid=(1,), out_shap...  31.8 us
    unnamed x14, local copies, waits for them, and re-layouts  6.28 us

profile of v4, /device:TPU:0, one launch (start us, length us, event | category | flops | bytes accessed | tf_op | source)
XLA Modules:
  0.0 192.0 jit_solution(10594031528570940266)
XLA Ops:
  0.6 0.7 sqrt_bitcast_fusion.scale_hbm
  1.4 0.0 copy-start.1
  1.4 1.6 copy-done.1
  3.0 0.0 copy-start.2
  3.0 1.2 copy-done.2
  4.2 0.0 copy-start.3
  4.2 0.0 copy-start.4
  4.2 0.0 copy-start.5
  4.2 152.4 %shard_map.86.q_ref.k_ref.v_ref = bf16[3,2048,256]{2,1,0:T(8,128)(2,1)} custom-call(bf16[512,1024]{1,0:T(8,128)(2,1)S(1)} %copy-done.2, bf16[1024,1024]{1,0:T(8,128)(2,1)S(1)} %copy-done.1, bf16[1024,1024]{1,0:T(8,128)(2,1)} %key_ref.1, bf16[1024,1024]{1,0:T(8,128)(2,1)} %value_ref.1), custom_call_target="tpu_custom_call" | custom-call | tf_op jit(solution)/shard_map/pallas_call | solution.py:491
  156.6 0.0 copy-done.3
  156.6 0.0 copy-done.4
  156.6 0.0 copy-done.5
  156.7 0.0 copy-start
  156.7 1.9 copy-done
  158.5 31.8 %shard_map.87 = (bf16[512,1024]{1,0:T(8,128)(2,1)S(1)}, f32[16,256]{1,0:T(8,128)S(1)}) custom-call(bf16[3,2048,256]{2,1,0:T(8,128)(2,1)S(1)} %copy-done, bf16[3,2048,256]{2,1,0:T(8,128)(2,1)S(1)} %copy-done, bf16[3,2048,256]{2,1,0:T(8,128)(2,1)S(1)} %copy-done, f32[16,256]{1,0:T(8,128)S(1)} %bitcast.6, f32[16,256]{1,0:T(8,128)S(1)} %sqrt_bitcast_fusion.scale_hbm, ...), custom_call_target="tpu_custom_call" | custom-call | tf_op jit(solution)/shard_map/pallas_call | solution.py:246
  190.4 1.0 copy.11
  191.4 0.6 copy.12
Async XLA Ops:
  1.4 1.6 copy-start.1
  3.0 1.2 copy-start.2
  4.2 152.4 %copy-start.3 = (f32[256,16]{0,1:T(8,128)S(1)}, f32[256,16]{0,1:T(8,128)}, u32[]{:S(2)}) copy-start(f32[256,16]{0,1:T(8,128)} %param.11) | copy-start | bytes 49156
  4.2 152.4 %copy-start.4 = (f32[256,16]{0,1:T(8,128)S(1)}, f32[256,16]{0,1:T(8,128)}, u32[]{:S(2)}) copy-start(f32[256,16]{0,1:T(8,128)} %param.12) | copy-start | bytes 49156
  4.2 152.5 %copy-start.5 = (f32[256,16]{0,1:T(8,128)S(1)}, f32[256,16]{0,1:T(8,128)}, u32[]{:S(2)}) copy-start(f32[256,16]{0,1:T(8,128)} %param.13) | copy-start | bytes 49156
  156.7 1.9 copy-start

commit v5 on v4

--- a/solution.py
+++ b/solution.py
@@ -263,13 +263,13 @@
             dma((count, width // LANES)), dma((count, width // LANES)),
         ],
         compiler_params=pltpu.CompilerParams(
-            collective_id=1, has_side_effects=True, vmem_limit_bytes=32 * 2**20
+            collective_id=1, has_side_effects=True, vmem_limit_bytes=60 * 2**20
         ),
     )(rows, rows, rows, rate.T, mode_scale(rate).T, residue.T, carried.T)
     return gated, state.T
 
 
-PIECES = 2
+PIECES = 4
 
 
 def project_kernel(count, tokens_ref, query_ref, key_ref, value_ref, out_ref,
@@ -311,8 +311,8 @@
 
     def hop(block, p, way, source=None):
         here = token_block(block, chan, rep, p)
-        device = {"seq": seq + 1 if way == 0 else seq - 1}
-        return remote(here if source is None else source, here, hop_send.at[block, p, way], hop_recv.at[block, p], device)
+        device = {"seq": seq + way}
+        return remote(here if source is None else source, here, hop_send.at[block, p, (1 - way) // 2], hop_recv.at[block, p], device)
 
     def side(block, p, source=None):
         here = token_block(block, chan, rep, p)
@@ -353,11 +353,17 @@
         there = weight_block(block, m, 1 - part)
         return remote(there, there, part_send.at[block, m], part_recv.at[block, m], {"parts": 1 - part})
 
+    inward = 1 - 2 * ((2 * seq) // count)
+
+    def inside(other):
+        return (other >= 0) & (other < count)
+
     def sources(distance):
-        return ((seq >= distance, seq - distance, 0), (seq + distance < count, seq + distance, 1))
+        near, far = seq - inward * distance, seq + inward * distance
+        return ((inside(near), near, inward), (inside(far), far, -inward))
 
     def has_next(way):
-        return seq + 1 < count if way == 0 else seq >= 1
+        return inside(seq + way)
 
     def send_weights(distance):
         for there, other, _ in sources(distance):
@@ -393,7 +399,7 @@
     for distance in range(1, count):
         send_weights(distance)
     for p in range(PIECES):
-        for way in range(2):
+        for way in (1, -1):
             @pl.when(has_next(way))
             def _():
                 hop(seq, p, way, own_piece(p)).start()
@@ -436,8 +442,8 @@
                     project(other)
 
     for distance in range(1, count):
-        for p in range(PIECES):
-            for there, other, way in sources(distance):
+        for there, other, way in sources(distance):
+            for p in range(PIECES):
                 @pl.when(there)
                 def _():
                     hop(other, p, way).wait_recv()
@@ -458,7 +464,7 @@
     finish(count - 1)
 
     for p in range(PIECES):
-        for way in range(2):
+        for way in (1, -1):
             @pl.when(has_next(way))
             def _():
                 hop(seq, p, way, own_piece(p)).wait_send()
@@ -504,7 +510,7 @@
             dma((count, 3)), dma((count, 3)),
         ],
         compiler_params=pltpu.CompilerParams(
-            collective_id=0, has_side_effects=True, vmem_limit_bytes=50 * 2**20
+            collective_id=0, has_side_effects=True, vmem_limit_bytes=63 * 2**20
         ),
     )(tokens, w_query, w_key, w_value)
 

time: 193 us -> 186 us (0.964)
  Pallas kernels: 184 us -> 179 us
  local copies, waits for them, and re-layouts: 6.28 us -> 2.88 us
    pallas_call x1, Pallas kernels: 31.8 us -> 25.9 us  [gated_scan(): pl.pallas_call(functools.partial(scan_kernel, count), grid=(1,), out_shap...]
    unnamed x14 -> x4, local copies, waits for them, and re-layouts: 6.28 us -> 2.88 us
where the time goes in v5:
time: 186 us; the launch traced here: 184 us
  Pallas kernels  179 us (96%)
  local copies, waits for them, and re-layouts  2.88 us (2%)
    pallas_call x1, Pallas kernels, project_all(): pl.pallas_call(functools.partial(project_kernel, count), out_shape=jax.Sh...  153 us
    pallas_call x1, Pallas kernels, gated_scan(): pl.pallas_call(functools.partial(scan_kernel, count), grid=(1,), out_shap...  25.9 us

profile of v5, /device:TPU:0, one launch (start us, length us, event | category | flops | bytes accessed | tf_op | source)
XLA Modules:
  0.0 184.2 jit_solution(18199856473558594193)
XLA Ops:
  0.6 1.3 sqrt_bitcast_fusion.scale_hbm
  2.0 153.4 %shard_map.86.q_ref.k_ref.v_ref = bf16[3,2048,256]{2,1,0:T(8,128)(2,1)} custom-call(bf16[512,1024]{1,0:T(8,128)(2,1)} %tokens_ref.1, bf16[1024,1024]{1,0:T(8,128)(2,1)} %query_ref.1, bf16[1024,1024]{1,0:T(8,128)(2,1)} %key_ref.1, bf16[1024,1024]{1,0:T(8,128)(2,1)} %value_ref.1), custom_call_target="tpu_custom_call" | custom-call | tf_op jit(solution)/shard_map/pallas_call | solution.py:497
  155.4 25.9 %shard_map.87 = (bf16[512,1024]{1,0:T(8,128)(2,1)}, f32[16,256]{1,0:T(8,128)}) custom-call(bf16[3,2048,256]{2,1,0:T(8,128)(2,1)} %shard_map.86.q_ref.k_ref.v_ref, bf16[3,2048,256]{2,1,0:T(8,128)(2,1)} %shard_map.86.q_ref.k_ref.v_ref, bf16[3,2048,256]{2,1,0:T(8,128)(2,1)} %shard_map.86.q_ref.k_ref.v_ref, f32[16,256]{1,0:T(8,128)} %bitcast.6, ...), custom_call_target="tpu_custom_call" | custom-call | tf_op jit(solution)/shard_map/pallas_call | solution.py:246
  181.3 0.0 copy-start
  181.3 2.3 %copy.11 = bf16[512,1024]{1,0:T(8,128)(2,1)} copy(bf16[512,1024]{1,0:T(8,128)(2,1)} %get-tuple-element.8) | data formatting | bytes 2097152
  183.6 0.0 copy-done
  183.6 0.6 copy.12
Async XLA Ops:
  181.3 2.3 %copy-start = (f32[16,256]{1,0:T(8,128)S(1)}, f32[16,256]{1,0:T(8,128)}, u32[]{:S(2)}) copy-start(f32[16,256]{1,0:T(8,128)} %get-tuple-element.5) | copy-start | bytes 49156
